TPU v7x, 32 devices: a whole 2x2x4 slice. The times are simulated.
32 devices in a mesh: seq: 8 (over z, x), tp: 4 (over y, core).
Axes of the slice: x: 2, y: 2, z: 4, core: 2. Of those that a mesh axis runs over, the one named last changes fastest.
Arguments:
- tokens_in: bfloat16 [4, 16, 1024], replicated, may hold values from -6 to 6
- key_cache: bfloat16 [16, 2048, 1024], P(None, 'seq', 'tp'), may hold values from -6 to 6
- value_cache: bfloat16 [16, 2048, 1024], P(None, 'seq', 'tp'), may hold values from -6 to 6
- cache_len: int32 [16], replicated, may hold values from 1 to 2048, as said below
- bucket_table: int32 [2052], replicated, may hold values from 0 to 31, as said below
- rel_bias: float32 [32, 16], P(None, 'tp'), may hold values from -4 to 283
- attn_gain: float32 [1024], replicated, may hold values from 0.1 to 1.9
- moe_gain: float32 [1024], replicated, may hold values from 0.1 to 1.9
- w_qkv: bfloat16 [3, 1024, 1024], P(None, None, 'tp'), may hold values from -0.1875 to 0.1875
- w_out: bfloat16 [1024, 1024], P('tp'), may hold values from -0.1875 to 0.1875
- router: bfloat16 [1024, 16], replicated, may hold values from -0.1875 to 0.1875
- expert_choice: int32 [4, 16, 2], replicated, may hold values from 0 to 15, all different within a row
- w_gate_up: bfloat16 [2, 45056, 1024], P(None, ('seq', 'tp')), may hold values from -0.1875 to 0.1875
- w_down: bfloat16 [45056, 1024], P(('seq', 'tp')), may hold values from -0.109375 to 0.109375
Outputs:
- layer_out: bfloat16 [4, 16, 1024], replicated
Inputs may be any that keep to these rules, and one draw needn't show every extreme that they name: Request r's cache holds its positions 0 to cache_len[r] - 1; some request holds exactly 2048. `bucket_table`: non-decreasing in the distance, 0 at distance 0. `expert_choice`: the 2 experts of a token differ.
All inputs are finite; a program needn't handle non-finite values.
Results may differ from a plain program's by a relative error of at most 0.012.
Values sent between devices are 32-bit elements; how exact they have to be, the bound alone decides.
No kernel may reach another device: no remote copies, remote signals or barrier semaphores. Data moves between devices by JAX's collectives and lax.ppermute only.
A program may use at most 64 MiB of HBM per device.

v0:
```python
import jax
import jax.numpy as jnp
from jax import lax
from jax.sharding import PartitionSpec as P

HEAD_DIM = 64
FF = 2816
NEG = -1e30
EPS = 1e-06


def rms_scale(values, gain_vec):
    return values * lax.rsqrt(jnp.mean(values * values, axis=-1, keepdims=True) + EPS) * gain_vec


def on_device(
    tokens_in,
    key_cache,
    value_cache,
    cache_len,
    bucket_table,
    rel_bias,
    attn_gain,
    moe_gain,
    w_qkv,
    w_out,
    router,
    expert_choice,
    w_gate_up,
    w_down,
):
    steps_all, requests, model_width = tokens_in.shape
    cache_rows = key_cache.shape[1]
    heads_local = key_cache.shape[2] // HEAD_DIM
    table_len = bucket_table.shape[0]
    num_buckets = rel_bias.shape[0]
    num_experts = router.shape[1]
    hidden_local = w_down.shape[0]
    bucket_ids = jnp.arange(num_buckets, dtype=jnp.int32)

    def bias_lookup(buckets, pattern):
        onehot = (buckets[..., None] == bucket_ids).astype(jnp.float32)
        return jnp.einsum(pattern, onehot, rel_bias, precision=lax.Precision.HIGHEST)

    normed = rms_scale(tokens_in.astype(jnp.float32), attn_gain).astype(jnp.bfloat16)
    projected = jnp.einsum(
        "srd,kdf->ksrf", normed, w_qkv, preferred_element_type=jnp.float32
    ).astype(jnp.bfloat16)
    head_shape = (steps_all, requests, heads_local, HEAD_DIM)
    queries = projected[0].reshape(head_shape)
    fresh_keys = projected[1].reshape(head_shape)
    fresh_values = projected[2].reshape(head_shape)
    keys_heads = key_cache.reshape(requests, cache_rows, heads_local, HEAD_DIM)
    values_heads = value_cache.reshape(requests, cache_rows, heads_local, HEAD_DIM)
    positions = lax.axis_index("seq") * cache_rows + jnp.arange(cache_rows, dtype=jnp.int32)
    live_rows = positions[None, :] < cache_len[:, None]

    def cache_part(query_blk, step_ids, keys_blk, vals_blk, lens_blk, live_blk):
        scores = jnp.einsum(
            "srhd,rchd->srhc", query_blk, keys_blk, preferred_element_type=jnp.float32
        )
        distance = lens_blk[None, :, None] + step_ids[:, None, None] - positions[None, None, :]
        buckets = jnp.take(bucket_table, jnp.clip(distance, 0, table_len - 1))
        scores = scores + bias_lookup(buckets, "srcb,bh->srhc")
        usable = live_blk[None, :, None, :]
        scores = jnp.where(usable, scores, NEG)
        maxima = jnp.max(scores, axis=-1)
        weights = jnp.where(usable, jnp.exp(scores - maxima[..., None]), 0.0)
        summed = jnp.einsum(
            "srhc,rchd->srhd", weights, vals_blk, preferred_element_type=jnp.float32
        )
        return (maxima, jnp.sum(weights, axis=-1), summed)

    def attend_cache(query_blk, step_ids):
        return cache_part(query_blk, step_ids, keys_heads, values_heads, cache_len, live_rows)

    def merge_cache(maxima, totals, summed):
        overall = lax.pmax(maxima, "seq")
        factor = jnp.exp(maxima - overall)
        totals, summed = lax.psum((totals * factor, summed * factor[..., None]), "seq")
        return (overall, totals, summed)

    def attend_recent(query_blk, step_ids):
        scores = jnp.einsum(
            "srhd,jrhd->srhj", query_blk, fresh_keys, preferred_element_type=jnp.float32
        )
        distance = step_ids[:, None] - jnp.arange(steps_all, dtype=jnp.int32)[None, :]
        buckets = jnp.take(bucket_table, jnp.clip(distance, 0, table_len - 1))
        scores = scores + bias_lookup(buckets, "sjb,bh->shj")[:, None]
        usable = (distance >= 0)[:, None, None, :]
        scores = jnp.where(usable, scores, NEG)
        maxima = jnp.max(scores, axis=-1)
        weights = jnp.where(usable, jnp.exp(scores - maxima[..., None]), 0.0)
        summed = jnp.einsum(
            "srhj,jrhd->srhd", weights, fresh_values, preferred_element_type=jnp.float32
        )
        return (maxima, jnp.sum(weights, axis=-1), summed)

    first_col = (lax.axis_index("seq") * lax.axis_size("tp") + lax.axis_index("tp")) * hidden_local
    col_expert = (first_col + jnp.arange(hidden_local, dtype=jnp.int32)) // FF
    owner = (col_expert[None, :] == jnp.arange(num_experts, dtype=jnp.int32)[:, None]).astype(
        jnp.float32
    )

    def layer(start, step_count):
        step_ids = jnp.arange(start, start + step_count, dtype=jnp.int32)
        query_blk = queries[start : start + step_count]
        cache_max, cache_tot, cache_sum = merge_cache(*attend_cache(query_blk, step_ids))
        new_max, new_tot, new_sum = attend_recent(query_blk, step_ids)
        joint = jnp.maximum(cache_max, new_max)
        scale_cache = jnp.exp(cache_max - joint)
        scale_new = jnp.exp(new_max - joint)
        totals = cache_tot * scale_cache + new_tot * scale_new
        summed = cache_sum * scale_cache[..., None] + new_sum * scale_new[..., None]
        attended = (
            (summed / totals[..., None])
            .reshape(step_count, requests, heads_local * HEAD_DIM)
            .astype(jnp.bfloat16)
        )
        partial_value = jnp.einsum(
            "srf,fd->srd", attended, w_out, preferred_element_type=jnp.float32
        )
        mid = tokens_in[start : start + step_count].astype(jnp.float32) + lax.psum(
            partial_value, "tp"
        )
        moe_in = rms_scale(mid, moe_gain).astype(jnp.bfloat16)
        logits = jnp.einsum("srd,de->sre", moe_in, router, preferred_element_type=jnp.float32)
        picked = expert_choice[start : start + step_count][..., None] == jnp.arange(
            num_experts, dtype=jnp.int32
        )
        chosen = jnp.sum(jnp.where(picked, logits[:, :, None, :], 0.0), axis=-1)
        leading = jax.nn.sigmoid(chosen[..., 0] - chosen[..., 1])
        gate_pair = jnp.stack([leading, 1.0 - leading], axis=-1)
        per_expert = jnp.sum(jnp.where(picked, gate_pair[..., None], 0.0), axis=2)
        coef = jnp.einsum("sre,ef->srf", per_expert, owner, precision=lax.Precision.HIGHEST)
        gate_up = jnp.einsum("srd,kfd->ksrf", moe_in, w_gate_up, preferred_element_type=jnp.float32)
        hidden = (jax.nn.gelu(gate_up[0], approximate=True) * gate_up[1] * coef).astype(
            jnp.bfloat16
        )
        expert_part = jnp.einsum("srf,fd->srd", hidden, w_down, preferred_element_type=jnp.float32)
        mixture = lax.psum(expert_part, ("seq", "tp"))
        return (mid + mixture).astype(jnp.bfloat16)

    return layer(0, steps_all)


def solution(mesh):
    return jax.shard_map(
        on_device,
        mesh=mesh,
        in_specs=(
            P(),
            P(None, "seq", "tp"),
            P(None, "seq", "tp"),
            P(),
            P(),
            P(None, "tp"),
            P(),
            P(),
            P(None, None, "tp"),
            P("tp", None),
            P(),
            P(),
            P(None, ("seq", "tp"), None),
            P(("seq", "tp"), None),
        ),
        out_specs=P(),
        check_vma=False,
    )
```

profile of v0, /device:TPU:0, one launch (start us, length us, event | category | flops | bytes accessed | tf_op | source)
XLA Modules:
  0.0 400.7 jit_solution(13281460656458387013)
XLA Ops:
  6.5 0.8 iota_add_fusion.1
  7.4 0.8 broadcast_compare_fusion
  8.3 90.5 %gather_fusion = s32[16384]{0:T(1024)S(1)} fusion(s32[2052]{0:T(1024)S(1)} %copy-done.1, s32[16384]{0:T(1024)S(1)} %broadcast_clamp_fusion), kind=kCustom, calls=%fused_computation | custom fusion | bytes 196608 | tf_op jit(solution)/shard_map/jit(_take)/gather | solution.py:63
  99.2 1.8 fusion.23
  101.7 4.0 copy.81
  106.4 2.1 fusion.80
  108.6 38.8 %pmax.7 = f32[4,16,4]{0,2,1:T(4,128)S(1)} all-reduce(f32[4,16,4]{0,2,1:T(4,128)S(1)} %get-tuple-element.17), channel_id=1, replica_groups=mesh['seq'=8,'tp'=4] {'seq'}, use_global_device_ids=true, to_apply=%region_2.3 | all-reduce | flops 256 | bytes 2048 | tf_op jit(solution)/shard_map/pmax | solution.py:78
  147.7 3.9 copy.84
  151.7 3.0 fusion.16
  154.7 33.7 %psum.29 = f32[4,16,4]{0,2,1:T(4,128)} all-reduce(f32[4,16,4]{0,2,1:T(4,128)S(1)} %bitcast.133), channel_id=1, replica_groups=mesh['seq'=8,'tp'=4] {'seq'}, use_global_device_ids=true, to_apply=%region_6.7 | all-reduce | flops 256 | bytes 2048 | tf_op jit(solution)/shard_map/psum | solution.py:80
  190.4 1.2 fusion.81
  192.4 1.4 multiply_add_fusion
  193.9 1.5 reshape_squeeze.11
  195.3 26.5 %all-reduce.4.cloned.1.call-done = f32[4,16,4,64]{3,0,2,1:T(4,128)} async-done(((f32[4,16,4,64]{3,0,2,1:T(4,128)}), f32[4,16,4,64]{3,0,2,1:T(4,128)}) %all-reduce.4.cloned.1.call-update) | async-done | bytes 65552 | tf_op jit(solution)/shard_map/psum | solution.py:80
  221.9 1.4 fusion.22
  223.9 1.6 convert_element_type.36
  225.5 1.7 fusion.27
  227.2 31.3 %all-reduce.6.cloned.1.call-done = f32[4,16,1024]{2,1,0:T(8,128)} async-done(((f32[4,16,1024]{2,1,0:T(8,128)}), f32[4,16,1024]{2,1,0:T(8,128)}) %all-reduce.6.cloned.1.call-update) | async-done | bytes 262160 | tf_op jit(solution)/shard_map/psum | solution.py:123
  258.5 1.1 multiply_reduce_fusion
  259.6 1.1 multiply_convert_fusion
  260.7 4.5 %fusion.4 = f32[2,4,16,1408]{3,2,0,1:T(8,128)S(1)} fusion(bf16[2,1408,1024]{2,1,0:T(8,128)(2,1)} %param.26, bf16[4,16,1024]{2,1,0:T(8,128)(2,1)S(1)} %multiply_convert_fusion), kind=kOutput, calls=%fused_computation.6 | convolution fusion | flops 369098752 | bytes 6619136 | tf_op jit(solution)/shard_map/srd,kfd->ksrf/dot_general | solution.py:136
  266.1 1.3 fusion.2
  267.5 125.1 %all-reduce.8.cloned.1.call-done = f32[4,16,1024]{2,1,0:T(8,128)} async-done(((f32[4,16,1024]{2,1,0:T(8,128)}), f32[4,16,1024]{2,1,0:T(8,128)}) %all-reduce.8.cloned.1.call-update) | async-done | bytes 262160 | tf_op jit(solution)/shard_map/psum | solution.py:141
  392.5 1.6 add_convert_fusion
  (70 shorter events, 6.6 us)
Async XLA Ops:
  6.5 259.5 %copy-start = (bf16[1408,1024]{1,0:T(8,128)(2,1)S(1)}, bf16[1408,1024]{1,0:T(8,128)(2,1)}, u32[]{:S(2)}) copy-start(bf16[1408,1024]{1,0:T(8,128)(2,1)} %param.27) | copy-start | bytes 8650756
  6.5 1.8 copy-start.1
  6.5 215.3 %all-reduce.4.cloned.1.call-start = ((), (), s32[]{:S(2)}) async-start(), calls=%async_computation | async-start | bytes 262144 | tf_op jit(solution)/shard_map/psum | solution.py:80
  8.3 90.7 %copy-start.2 = (bf16[4,16,1024]{2,1,0:T(8,128)(2,1)S(1)}, bf16[4,16,1024]{2,1,0:T(8,128)(2,1)}, u32[]{:S(2)}) copy-start(bf16[4,16,1024]{2,1,0:T(8,128)(2,1)} %param.14) | copy-start | bytes 393220
  8.3 90.8 %copy-start.10 = (f32[1024]{0:T(1024)S(1)}, f32[1024]{0:T(1024)}, u32[]{:S(2)}) copy-start(f32[1024]{0:T(1024)} %param.20) | copy-start | bytes 12292
  101.7 4.7 %copy-start.6 = (bf16[4,16,4,64]{3,2,1,0:T(4,128)(2,1)}, bf16[4,16,4,64]{3,2,1,0:T(4,128)(2,1)S(1)}, u32[]{:S(2)}) copy-start(bf16[4,16,4,64]{3,2,1,0:T(4,128)(2,1)S(1)} %reshape_squeeze.9) | copy-start | bytes 98308
  101.7 4.0 copy-start.13
  147.4 4.2 %copy-start.5 = (f32[4,16,4]{0,2,1:T(4,128)}, f32[4,16,4]{0,2,1:T(4,128)S(1)}, u32[]{:S(2)}) copy-start(f32[4,16,4]{0,2,1:T(4,128)S(1)} %pmax.7) | copy-start | bytes 3076
  154.7 103.9 %all-reduce.6.cloned.1.call-start = ((), (), s32[]{:S(2)}) async-start(), calls=%async_computation.1 | async-start | bytes 524288 | tf_op jit(solution)/shard_map/psum | solution.py:123
  190.4 35.0 %copy-start.4 = (bf16[256,1024]{1,0:T(8,128)(2,1)S(1)}, bf16[256,1024]{1,0:T(8,128)(2,1)}, u32[]{:S(2)}) copy-start(bf16[256,1024]{1,0:T(8,128)(2,1)} %param.23) | copy-start | bytes 1572868
  191.6 0.7 copy-start.7
  191.6 0.8 copy-start.8
  221.9 37.8 %copy-start.12 = (f32[1024]{0:T(1024)S(1)}, f32[1024]{0:T(1024)}, u32[]{:S(2)}) copy-start(f32[1024]{0:T(1024)} %param.21) | copy-start | bytes 12292
  227.1 165.4 %all-reduce.8.cloned.1.call-start = ((), (), s32[]{:S(2)}) async-start(), calls=%async_computation.2 | async-start | bytes 524288 | tf_op jit(solution)/shard_map/psum | solution.py:141
  260.7 4.5 %copy-start.9 = (bf16[1024,16]{0,1:T(8,128)(2,1)S(1)}, bf16[1024,16]{0,1:T(8,128)(2,1)}, u32[]{:S(2)}) copy-start(bf16[1024,16]{0,1:T(8,128)(2,1)} %param.24) | copy-start | bytes 98308
  260.7 4.7 %copy-start.11 = (s32[4,16,2]{1,2,0:T(2,128)S(1)}, s32[4,16,2]{1,2,0:T(2,128)}, u32[]{:S(2)}) copy-start(s32[4,16,2]{1,2,0:T(2,128)} %param.25) | copy-start | bytes 1540
  266.1 126.5 %copy-start.3 = (f32[4,16,1024]{2,1,0:T(8,128)S(1)}, f32[4,16,1024]{2,1,0:T(8,128)}, u32[]{:S(2)}) copy-start(f32[4,16,1024]{2,1,0:T(8,128)} %all-reduce.6.cloned.1.call-done) | copy-start | bytes 786436
Sparse Core Ops, SparseCore 0:
  154.8 67.0 all-reduce.3
  227.3 31.2 all-reduce.5
  267.6 124.9 all-reduce.7
where the time goes:
time: 402 us; the launch traced here: 401 us
  waiting for transfers between devices  183 us (46%)
  local copies, waits for them, and re-layouts  105 us (26%)
  blocking collectives  72.5 us (18%)
  matrix products  18.5 us (5%)
  between operations  13.4 us (3%)
  other arithmetic  7.9 us (2%)
    psum x1, waiting for transfers between devices, layer(): mixture = lax.psum(expert_part, ('seq', 'tp'))  125 us
    gather x2, local copies, waits for them, and re-layouts, cache_part(): buckets = jnp.take(bucket_table, jnp.clip(distance, 0, table_len - 1))  90.6 us
    pmax x1, blocking collectives, merge_cache(): overall = lax.pmax(maxima, 'seq')  38.8 us
    psum x1, blocking collectives, merge_cache(): lax.psum((totals * factor, summed * factor[..., None]), 'seq')  33.7 us
    psum x1, waiting for transfers between devices, layer(): lax.psum(partial_value, 'tp')  31.3 us
    psum x1, waiting for transfers between devices, merge_cache(): lax.psum((totals * factor, summed * factor[..., None]), 'seq')  26.5 us
    unnamed x31, local copies, waits for them, and re-layouts  8.62 us
  transfers between devices with their start and end apart: 3, of which 3 were waited for; matrix products, arithmetic and copies ran while one was open for 2% of the time, Pallas kernels for 0%

commit v1 on v0

--- a/solution.py
+++ b/solution.py
@@ -138,7 +138,7 @@
             jnp.bfloat16
         )
         expert_part = jnp.einsum("srf,fd->srd", hidden, w_down, preferred_element_type=jnp.float32)
-        mixture = lax.psum(expert_part, ("seq", "tp"))
+        mixture = jnp.sum(lax.all_gather(expert_part, ("seq", "tp")), axis=0)
         return (mid + mixture).astype(jnp.bfloat16)
 
     return layer(0, steps_all)

time: 402 us -> 359 us (0.89)
  waiting for transfers between devices: 183 us -> 136 us
    psum x1 -> x0, waiting for transfers between devices: 125 us -> none  [layer(): mixture = lax.psum(expert_part, ('seq', 'tp'))]
    all_gather x0 -> x1, waiting for transfers between devices: none -> 77.7 us  [layer(): mixture = jnp.sum(lax.all_gather(expert_part, ('seq', 'tp')), axis=0)]
    reduce_sum x0 -> x1, other arithmetic: none -> 4.02 us  [layer(): mixture = jnp.sum(lax.all_gather(expert_part, ('seq', 'tp')), axis=0)]
    unnamed x31 -> x29, local copies, waits for them, and re-layouts: 8.62 us -> 8.61 us
where the time goes in v1:
time: 359 us; the launch traced here: 358 us
  waiting for transfers between devices  136 us (38%)
  local copies, waits for them, and re-layouts  105 us (29%)
  blocking collectives  72.4 us (20%)
  matrix products  19.2 us (5%)
  between operations  13.4 us (4%)
  other arithmetic  11.9 us (3%)
    gather x2, local copies, waits for them, and re-layouts, cache_part(): buckets = jnp.take(bucket_table, jnp.clip(distance, 0, table_len - 1))  90.6 us
    all_gather x1, waiting for transfers between devices, layer(): mixture = jnp.sum(lax.all_gather(expert_part, ('seq', 'tp')), axis=0)  77.7 us
    pmax x1, blocking collectives, merge_cache(): overall = lax.pmax(maxima, 'seq')  38.8 us
    psum x1, blocking collectives, merge_cache(): lax.psum((totals * factor, summed * factor[..., None]), 'seq')  33.6 us
    psum x1, waiting for transfers between devices, layer(): lax.psum(partial_value, 'tp')  31.3 us
    psum x1, waiting for transfers between devices, merge_cache(): lax.psum((totals * factor, summed * factor[..., None]), 'seq')  26.6 us
    unnamed x29, local copies, waits for them, and re-layouts  8.61 us
  transfers between devices with their start and end apart: 3, of which 3 were waited for; matrix products, arithmetic and copies ran while one was open for 2% of the time, Pallas kernels for 0%

profile of v1, /device:TPU:0, one launch (start us, length us, event | category | flops | bytes accessed | tf_op | source)
XLA Modules:
  0.0 358.0 jit_solution(595871910778865491)
XLA Ops:
  7.4 1.1 fusion.37
  9.4 90.5 %gather_fusion = s32[16384]{0:T(1024)S(1)} fusion(s32[2052]{0:T(1024)S(1)} %copy-done.1, s32[16384]{0:T(1024)S(1)} %broadcast_clamp_fusion), kind=kCustom, calls=%fused_computation | custom fusion | bytes 196608 | tf_op jit(solution)/shard_map/jit(_take)/gather | solution.py:63
  100.1 1.8 fusion.23
  102.7 4.0 %copy.81 = bf16[16,256,256]{1,2,0:T(8,128)(2,1)} copy(bf16[16,256,256]{2,1,0:T(8,128)(2,1)} %param.15) | data formatting | bytes 4194304 | tf_op args[1]
  107.4 2.1 fusion.80
  109.5 38.8 %pmax.7 = f32[4,16,4]{0,2,1:T(4,128)S(1)} all-reduce(f32[4,16,4]{0,2,1:T(4,128)S(1)} %get-tuple-element.17), channel_id=1, replica_groups=mesh['seq'=8,'tp'=4] {'seq'}, use_global_device_ids=true, to_apply=%region_2.3 | all-reduce | flops 256 | bytes 2048 | tf_op jit(solution)/shard_map/pmax | solution.py:78
  148.6 3.9 %copy.84 = bf16[16,256,256]{1,2,0:T(8,128)(2,1)} copy(bf16[16,256,256]{2,1,0:T(8,128)(2,1)} %param.16) | data formatting | bytes 4194304 | tf_op args[2]
  152.6 3.0 fusion.16
  157.6 33.6 %psum.22 = f32[4,16,4]{0,2,1:T(4,128)} all-reduce(f32[4,16,4]{0,2,1:T(4,128)S(1)} %bitcast.134), channel_id=1, replica_groups=mesh['seq'=8,'tp'=4] {'seq'}, use_global_device_ids=true, to_apply=%region_6.7 | all-reduce | flops 256 | bytes 2048 | tf_op jit(solution)/shard_map/psum | solution.py:80
  191.3 1.2 fusion.81
  193.2 1.4 multiply_add_fusion
  194.7 1.5 reshape_squeeze.11
  196.2 26.6 %all-reduce.3.cloned.1.call-done = f32[4,16,4,64]{3,0,2,1:T(4,128)} async-done(((f32[4,16,4,64]{3,0,2,1:T(4,128)}), f32[4,16,4,64]{3,0,2,1:T(4,128)}) %all-reduce.3.cloned.1.call-update) | async-done | bytes 65552 | tf_op jit(solution)/shard_map/psum | solution.py:80
  222.7 1.4 fusion.22
  224.8 1.6 convert_element_type.36
  226.4 1.7 fusion.27
  228.1 31.3 %all-reduce.5.cloned.1.call-done = f32[4,16,1024]{2,1,0:T(8,128)} async-done(((f32[4,16,1024]{2,1,0:T(8,128)}), f32[4,16,1024]{2,1,0:T(8,128)}) %all-reduce.5.cloned.1.call-update) | async-done | bytes 262160 | tf_op jit(solution)/shard_map/psum | solution.py:123
  259.4 1.1 multiply_reduce_fusion
  260.5 1.1 multiply_convert_fusion
  261.6 0.9 fusion.66
  262.8 4.5 %fusion.4 = f32[2,4,16,1408]{3,2,0,1:T(8,128)S(1)} fusion(bf16[2,1408,1024]{2,1,0:T(8,128)(2,1)} %param.26, bf16[4,16,1024]{2,1,0:T(8,128)(2,1)S(1)} %multiply_convert_fusion), kind=kOutput, calls=%fused_computation.6 | convolution fusion | flops 369098752 | bytes 6619136 | tf_op jit(solution)/shard_map/srd,kfd->ksrf/dot_general | solution.py:136
  267.7 1.3 fusion.2
  269.1 77.7 %all-gather.3.cloned.1.call-done = f32[128,16,1024]{2,1,0:T(8,128)} async-done(((f32[4,16,1024]{2,1,0:T(8,128)}), f32[128,16,1024]{2,1,0:T(8,128)}) %all-gather.3.cloned.1.call-update) | async-done | bytes 8388624 | tf_op jit(solution)/shard_map/all_gather | solution.py:141
  346.8 4.0 %reduce_sum.69 = f32[4,16,1024]{2,1,0:T(8,128)S(1)} reduce(f32[32,4,16,1024]{3,2,1,0:T(8,128)} %bitcast.126, f32[]{:T(128)} %constant.26.clone.1), dimensions={0}, to_apply=%region_12.13 | reduce | flops 2031616 | bytes 8650756 | tf_op jit(solution)/shard_map/reduce_sum | solution.py:141
  (69 shorter events, 8.5 us)
Async XLA Ops:
  6.5 261.2 %copy-start = (bf16[1408,1024]{1,0:T(8,128)(2,1)S(1)}, bf16[1408,1024]{1,0:T(8,128)(2,1)}, u32[]{:S(2)}) copy-start(bf16[1408,1024]{1,0:T(8,128)(2,1)} %param.27) | copy-start | bytes 8650756
  6.5 2.8 copy-start.1
  6.5 216.2 %all-reduce.3.cloned.1.call-start = ((), (), s32[]{:S(2)}) async-start(), calls=%async_computation | async-start | bytes 262144 | tf_op jit(solution)/shard_map/psum | solution.py:80
  9.4 90.7 %copy-start.2 = (bf16[4,16,1024]{2,1,0:T(8,128)(2,1)S(1)}, bf16[4,16,1024]{2,1,0:T(8,128)(2,1)}, u32[]{:S(2)}) copy-start(bf16[4,16,1024]{2,1,0:T(8,128)(2,1)} %param.14) | copy-start | bytes 393220
  9.4 90.7 %copy-start.9 = (f32[1024]{0:T(1024)S(1)}, f32[1024]{0:T(1024)}, u32[]{:S(2)}) copy-start(f32[1024]{0:T(1024)} %param.20) | copy-start | bytes 12292
  102.6 4.7 %copy-start.6 = (bf16[4,16,4,64]{3,2,1,0:T(4,128)(2,1)}, bf16[4,16,4,64]{3,2,1,0:T(4,128)(2,1)S(1)}, u32[]{:S(2)}) copy-start(bf16[4,16,4,64]{3,2,1,0:T(4,128)(2,1)S(1)} %reshape_squeeze.9) | copy-start | bytes 98308
  102.6 4.0 %copy-start.12 = (f32[32,4]{0,1:T(4,128)S(1)}, f32[32,4]{0,1:T(4,128)}, u32[]{:S(2)}) copy-start(f32[32,4]{0,1:T(4,128)} %param.19) | copy-start | bytes 1540
  148.3 4.2 %copy-start.5 = (f32[4,16,4]{0,2,1:T(4,128)}, f32[4,16,4]{0,2,1:T(4,128)S(1)}, u32[]{:S(2)}) copy-start(f32[4,16,4]{0,2,1:T(4,128)S(1)} %pmax.7) | copy-start | bytes 3076
  155.6 103.9 %all-reduce.5.cloned.1.call-start = ((), (), s32[]{:S(2)}) async-start(), calls=%async_computation.1 | async-start | bytes 524288 | tf_op jit(solution)/shard_map/psum | solution.py:123
  191.3 35.1 %copy-start.4 = (bf16[256,1024]{1,0:T(8,128)(2,1)S(1)}, bf16[256,1024]{1,0:T(8,128)(2,1)}, u32[]{:S(2)}) copy-start(bf16[256,1024]{1,0:T(8,128)(2,1)} %param.23) | copy-start | bytes 1572868
  192.4 0.7 copy-start.7
  192.5 0.8 copy-start.8
  222.7 37.8 %copy-start.11 = (f32[1024]{0:T(1024)S(1)}, f32[1024]{0:T(1024)}, u32[]{:S(2)}) copy-start(f32[1024]{0:T(1024)} %param.21) | copy-start | bytes 12292
  222.7 39.8 %copy-start.10 = (s32[4,16,2]{1,2,0:T(2,128)S(1)}, s32[4,16,2]{1,2,0:T(2,128)}, u32[]{:S(2)}) copy-start(s32[4,16,2]{1,2,0:T(2,128)} %param.25) | copy-start | bytes 1540
  228.0 118.7 %all-gather.3.cloned.1.call-start = ((), (), s32[]{:S(2)}) async-start(), calls=%async_computation.2 | async-start | bytes 8650752 | tf_op jit(solution)/shard_map/all_gather | solution.py:141
  346.8 4.0 %copy-start.3 = (f32[4,16,1024]{2,1,0:T(8,128)S(1)}, f32[4,16,1024]{2,1,0:T(8,128)}, u32[]{:S(2)}) copy-start(f32[4,16,1024]{2,1,0:T(8,128)} %all-reduce.5.cloned.1.call-done) | copy-start | bytes 786436
Sparse Core Ops, SparseCore 0:
  155.7 67.0 all-reduce.2
  228.2 31.2 all-reduce.4
  269.2 77.5 all-gather.2
